TPU v7x, 32 devices: a whole 2x2x4 slice. The times are simulated.
32 devices in a mesh: expo: 4 (over y, x), fp: 8 (over z, core).
Axes of the slice: x: 2, y: 2, z: 4, core: 2. Of those that a mesh axis runs over, the one named last changes fastest.
Arguments:
- raw_pixels: bfloat16 [4, 2048, 2048], P('expo', 'fp'), may hold values from -6 to 6
- kernel_bank: bfloat16 [8, 2, 41], replicated, may hold values from -1 to 1
- kernel_ids: int32 [4, 8], P('expo', 'fp'), may hold values from 0 to 7
- inv_var: float32 [4, 8], P('expo', 'fp'), may hold values from 0.3 to 3
- gap_start: int32 [4, 8], P('expo', 'fp'), may hold values from 0 to 224
- warp_tile: int32 [4, 2048, 16, 1], P('expo', 'fp'), may hold values from 0 to 31; in each aligned block of 4096 rows (0 to 4095, 4096 to 8191, ..., all dimensions but the last counted through in order) at most 256 rows name the same one
- warp_offset: int32 [4, 2048, 16], P('expo', 'fp'), may hold values from 0 to 4095
Outputs:
- coadd_image: float32 [32, 4096, 128], P(('expo', 'fp'))
- coadd_weight: float32 [32, 4096], P(('expo', 'fp'))
Inputs may be any that keep to these rules, and one draw needn't show every extreme that they name: `warp_tile`: among the 4096 row segments of one exposure's CCD window (256 pixel rows of 16 segments each), at most 256 go to one tile, and in some windows exactly 256 do.
All inputs are finite; a program needn't handle non-finite values.
Results may differ from a plain program's by a relative error of at most 0.006.
Values may be sent and summed in bfloat16 or wider, within the bound.
No kernel may reach another device: no remote copies, remote signals or barrier semaphores. Data moves between devices by JAX's collectives and lax.ppermute only.
A program may use at most 64 MiB of HBM per device.

v0:
```python
import math

import jax
import jax.numpy as jnp
from jax import lax
from jax.sharding import PartitionSpec as P

GAP = 32


def padded_2(shard, sides, width):
    for axis, dim in sides:
        size, length = (lax.axis_size(axis), shard.shape[dim])
        up = [(i, (i + 1) % size) for i in range(size - 1)]
        down = [(j, i) for i, j in up]
        last = lax.slice_in_dim(shard, length - width, length, axis=dim)
        first = lax.slice_in_dim(shard, 0, width, axis=dim)
        before = lax.ppermute(last, axis, up)
        after = lax.ppermute(first, axis, down)
        shard = jnp.concatenate([before, shard, after], axis=dim)
    return shard


def toeplitz(tap_table, offset):
    tap_total = tap_table.shape[1]
    row_pos = jnp.arange(128)[:, None]
    col_pos = jnp.arange(128)[None, :]
    where_tap = offset + row_pos - col_pos
    band = (where_tap[None, :, :] == jnp.arange(tap_total)[:, None, None]).astype(jnp.bfloat16)
    built = jnp.einsum("et,tab->eab", tap_table, band, preferred_element_type=jnp.float32)
    return built.astype(jnp.bfloat16)


def body(raw_pixels, kernel_bank, kernel_ids, inv_var, gap_start, warp_tile, warp_offset):
    e_dev, row_count, col_count = raw_pixels.shape
    block_width = 128
    half_taps = kernel_bank.shape[2] // 2
    row_blocks = row_count // block_width
    col_blocks = col_count // block_width
    selector = (kernel_ids == jnp.arange(kernel_bank.shape[0])[None, :]).astype(jnp.float32)
    tap_table = jnp.einsum("ek,kst->est", selector, kernel_bank.astype(jnp.float32)).astype(
        jnp.bfloat16
    )
    padded = padded_2(raw_pixels, (("fp", 1),), half_taps)
    padded = jnp.pad(padded, ((0, 0), (0, block_width - 2 * half_taps), (0, 0)))
    stacked = padded.reshape(e_dev, row_blocks + 1, block_width, col_count)
    upper_matrix = toeplitz(tap_table[:, 0], 0)
    lower_matrix = toeplitz(tap_table[:, 0], block_width)
    vertical = jnp.einsum(
        "eiac,eab->eibc", stacked[:, :row_blocks], upper_matrix, preferred_element_type=jnp.float32
    )
    vertical = vertical + jnp.einsum(
        "eiac,eab->eibc", stacked[:, 1:], lower_matrix, preferred_element_type=jnp.float32
    )
    vertical = vertical.reshape(e_dev, row_count, col_blocks, block_width).astype(jnp.bfloat16)
    framed = jnp.pad(vertical, ((0, 0), (0, 0), (1, 1), (0, 0)))
    filtered = jnp.zeros((e_dev, row_count, col_blocks, block_width), jnp.float32)
    for block_shift in (-1, 0, 1):
        matrix = toeplitz(tap_table[:, 1], block_width * block_shift + half_taps)
        filtered = filtered + jnp.einsum(
            "erja,eab->erjb",
            framed[:, :, 1 + block_shift : 1 + block_shift + col_blocks],
            matrix,
            preferred_element_type=jnp.float32,
        )
    convolved = filtered.astype(jnp.bfloat16).reshape(e_dev, row_count * col_blocks, block_width)
    row_index = jnp.arange(row_count)[None, :]
    in_gap = (row_index >= gap_start) & (row_index < gap_start + GAP)
    row_weight = jnp.where(in_gap, jnp.zeros((), jnp.float32), inv_var)
    piece_weight = jnp.broadcast_to(row_weight[:, :, None], (e_dev, row_count, col_blocks)).reshape(
        e_dev, -1
    )
    targets = warp_tile.reshape(e_dev, -1)
    offsets = warp_offset.reshape(e_dev, -1)
    pieces = targets.shape[1]
    devices = lax.axis_size("expo") * lax.axis_size("fp")
    capacity = max(2, 2 * pieces // devices)
    owner_hot = (targets[:, :, None] == jnp.arange(devices)[None, None, :]).astype(jnp.bfloat16)
    piece_groups = pieces // 128
    grouped_hot = owner_hot.reshape(e_dev, piece_groups, 128, devices)
    strictly_lower = (jnp.arange(128)[:, None] > jnp.arange(128)[None, :]).astype(jnp.bfloat16)
    inside_rank = jnp.einsum(
        "ab,enbd->enad", strictly_lower, grouped_hot, preferred_element_type=jnp.float32
    )
    group_totals = jnp.sum(grouped_hot.astype(jnp.float32), axis=2)
    group_before = jnp.cumsum(group_totals, axis=1) - group_totals
    rank_value = jnp.sum(
        grouped_hot.astype(jnp.float32) * (inside_rank + group_before[:, :, None, :]), axis=3
    )
    destination = targets * capacity + rank_value.reshape(e_dev, pieces).astype(jnp.int32)
    send_slots = devices * capacity
    send_block = math.gcd(send_slots, 1024)

    def pack_block(block_number):
        slot_index = block_number * send_block + jnp.arange(send_block)
        matched = destination[:, None, :] == slot_index[None, :, None]
        values = jnp.einsum(
            "ebp,epc->ebc",
            matched.astype(jnp.bfloat16),
            convolved,
            preferred_element_type=jnp.float32,
        ).astype(jnp.bfloat16)
        slot_offsets = jnp.sum(jnp.where(matched, offsets[:, None, :], 0), axis=2)
        slot_weights = jnp.sum(
            jnp.where(matched, piece_weight[:, None, :], jnp.zeros((), jnp.float32)), axis=2
        )
        return (values, slot_offsets, slot_weights)

    packed_values, packed_offsets, packed_weights = lax.map(
        pack_block, jnp.arange(send_slots // send_block)
    )
    send_values = jnp.transpose(
        jnp.transpose(packed_values, (1, 0, 2, 3)).reshape(e_dev, devices, capacity, block_width),
        (1, 0, 2, 3),
    )
    send_offsets = jnp.transpose(
        jnp.transpose(packed_offsets, (1, 0, 2)).reshape(e_dev, devices, capacity), (1, 0, 2)
    )
    send_weights = jnp.transpose(
        jnp.transpose(packed_weights, (1, 0, 2)).reshape(e_dev, devices, capacity), (1, 0, 2)
    )
    got_values, got_offsets, got_weights = (
        lax.all_to_all(send_values, ("expo", "fp"), split_axis=0, concat_axis=0, tiled=True),
        lax.all_to_all(send_offsets, ("expo", "fp"), split_axis=0, concat_axis=0, tiled=True),
        lax.all_to_all(
            send_weights.astype(jnp.bfloat16),
            ("expo", "fp"),
            split_axis=0,
            concat_axis=0,
            tiled=True,
        ).astype(send_weights.dtype),
    )
    flat_values = got_values.reshape(-1, block_width)
    flat_offsets = got_offsets.reshape(-1)
    flat_weights = got_weights.reshape(-1)
    products = flat_weights[:, None] * flat_values.astype(jnp.float32)
    upper_part = products.astype(jnp.bfloat16)
    lower_part = (products - upper_part.astype(jnp.float32)).astype(jnp.bfloat16)
    both_parts = jnp.concatenate([upper_part, lower_part], axis=1)
    sum_block_rows = math.gcd(pieces, 512)

    def sum_block(block_number):
        slot_index = block_number * sum_block_rows + jnp.arange(sum_block_rows)
        matched = slot_index[:, None] == flat_offsets[None, :]
        summed = jnp.dot(
            matched.astype(jnp.bfloat16), both_parts, preferred_element_type=jnp.float32
        )
        image_rows = summed[:, :block_width] + summed[:, block_width:]
        weight_rows = jnp.sum(
            jnp.where(matched, flat_weights[None, :], jnp.zeros((), jnp.float32)), axis=1
        )
        return (image_rows, weight_rows)

    image_blocks, weight_blocks = lax.map(sum_block, jnp.arange(pieces // sum_block_rows))
    weighted_sum = image_blocks.reshape(pieces, block_width)
    weight_sum = weight_blocks.reshape(pieces)
    coadd_image = weighted_sum / jnp.maximum(weight_sum, 1.0)[:, None]
    return (coadd_image[None], weight_sum[None])


def solution(mesh):
    in_specs = (
        P("expo", "fp", None),
        P(),
        P("expo", "fp"),
        P("expo", "fp"),
        P("expo", "fp"),
        P("expo", "fp", None, None),
        P("expo", "fp", None),
    )
    out_specs = (P(("expo", "fp"), None, None), P(("expo", "fp"), None))
    return jax.shard_map(body, mesh=mesh, in_specs=in_specs, out_specs=out_specs, check_vma=False)
```

profile of v0, /device:TPU:0, one launch (start us, length us, event | category | flops | bytes accessed | tf_op | source)
XLA Modules:
  0.0 239.7 jit_solution(9159352962510795056)
XLA Ops:
  0.6 1.0 fusion.78
  1.6 2.4 %collective-permute-start = (bf16[1,20,2048]{2,1,0:T(8,128)(2,1)S(1)}, bf16[1,20,2048]{2,1,0:T(8,128)(2,1)S(1)}, u32[]{:S(2)}, u32[]{:S(2)}) collective-permute-start(bf16[1,20,2048]{2,1,0:T(8,128)(2,1)S(1)} %get-tuple-element.183), channel_id=1, source_target_pairs={{0,1},{1,2},{2,3},{3,4},{4,5},{5,6},{6,7},{8,9},{9,10},{10,11},{11... | collective-permute-start | bytes 245768 | tf_op jit(solution)/shard_map/ppermute | solution.py:18
  4.0 1.3 collective-permute-start.1
  5.4 0.8 copy.31
  6.2 0.7 broadcast_multiply_fusion
  8.2 1.1 fusion.39
  9.8 1.1 fusion.37
  11.5 1.0 fusion.35
  13.0 1.0 fusion.33
  14.6 1.0 fusion.31
  21.2 0.7 copy.34
  21.9 71.0 %while.29 = (s32[]{:T(128)}, bf16[8,1,1024,128]{3,2,1,0:T(8,128)(2,1)}, s32[8,1,1024]{2,1,0:T(1,128)}, bf16[8,1,1024]{2,1,0:T(2,128)(2,1)S(1)}, s32[1,4096]{1,0:...) while((s32[]{:T(128)}, ...), condition=%wide.wide.region_6.7_spmd.clone, body=%wide.wide.region_3.6_spmd.clone.sunk | while | flops 1103232000 | bytes 1484949 | solution.py:109
  23.3 3.1 %fusion.102 = bf16[8,1,1024,128]{3,2,1,0:T(8,128)(2,1)} fusion(bf16[8,1,1024,128]{3,2,1,0:T(8,128)(2,1)} %get-tuple-element.338, s32[]{:T(128)} %get-tuple-element.337, s32[4096]{0:T(1024)S(1)} %bitcast.206, s32[1024]{0:T(1024)S(1)} %iota_add_fusion.10, bf16[1,4096,128]{2,1,0:T(8,128)(2,1)S(1)} %get-tuple-element.355), kind=kOutput, calls=%fused_computation.21.clone.clone.1 | convolution fusion | flops 1078067200 | bytes 1331712 | tf_op jit(solution)/shard_map/while/body/eval_jaxpr/ebp,epc->ebc/dot_general | solution.py:97
  26.6 1.8 fusion.104
  28.5 1.8 fusion.103
  30.3 0.6 constant_dynamic-update-slice_fusion.6
  32.1 3.1 %fusion.102 = bf16[8,1,1024,128]{3,2,1,0:T(8,128)(2,1)} fusion(bf16[8,1,1024,128]{3,2,1,0:T(8,128)(2,1)} %get-tuple-element.338, s32[]{:T(128)} %get-tuple-element.337, s32[4096]{0:T(1024)S(1)} %bitcast.206, s32[1024]{0:T(1024)S(1)} %iota_add_fusion.10, bf16[1,4096,128]{2,1,0:T(8,128)(2,1)S(1)} %get-tuple-element.355), kind=kOutput, calls=%fused_computation.21.clone.clone.1 | convolution fusion | flops 1078067200 | bytes 1331712 | tf_op jit(solution)/shard_map/while/body/eval_jaxpr/ebp,epc->ebc/dot_general | solution.py:97
  35.5 1.8 fusion.104
  37.3 1.8 fusion.103
  41.0 3.1 %fusion.102 = bf16[8,1,1024,128]{3,2,1,0:T(8,128)(2,1)} fusion(bf16[8,1,1024,128]{3,2,1,0:T(8,128)(2,1)} %get-tuple-element.338, s32[]{:T(128)} %get-tuple-element.337, s32[4096]{0:T(1024)S(1)} %bitcast.206, s32[1024]{0:T(1024)S(1)} %iota_add_fusion.10, bf16[1,4096,128]{2,1,0:T(8,128)(2,1)S(1)} %get-tuple-element.355), kind=kOutput, calls=%fused_computation.21.clone.clone.1 | convolution fusion | flops 1078067200 | bytes 1331712 | tf_op jit(solution)/shard_map/while/body/eval_jaxpr/ebp,epc->ebc/dot_general | solution.py:97
  44.3 1.8 fusion.104
  46.2 1.8 fusion.103
  49.8 3.1 %fusion.102 = bf16[8,1,1024,128]{3,2,1,0:T(8,128)(2,1)} fusion(bf16[8,1,1024,128]{3,2,1,0:T(8,128)(2,1)} %get-tuple-element.338, s32[]{:T(128)} %get-tuple-element.337, s32[4096]{0:T(1024)S(1)} %bitcast.206, s32[1024]{0:T(1024)S(1)} %iota_add_fusion.10, bf16[1,4096,128]{2,1,0:T(8,128)(2,1)S(1)} %get-tuple-element.355), kind=kOutput, calls=%fused_computation.21.clone.clone.1 | convolution fusion | flops 1078067200 | bytes 1331712 | tf_op jit(solution)/shard_map/while/body/eval_jaxpr/ebp,epc->ebc/dot_general | solution.py:97
  53.1 1.8 fusion.104
  55.0 1.8 fusion.103
  58.7 3.1 %fusion.102 = bf16[8,1,1024,128]{3,2,1,0:T(8,128)(2,1)} fusion(bf16[8,1,1024,128]{3,2,1,0:T(8,128)(2,1)} %get-tuple-element.338, s32[]{:T(128)} %get-tuple-element.337, s32[4096]{0:T(1024)S(1)} %bitcast.206, s32[1024]{0:T(1024)S(1)} %iota_add_fusion.10, bf16[1,4096,128]{2,1,0:T(8,128)(2,1)S(1)} %get-tuple-element.355), kind=kOutput, calls=%fused_computation.21.clone.clone.1 | convolution fusion | flops 1078067200 | bytes 1331712 | tf_op jit(solution)/shard_map/while/body/eval_jaxpr/ebp,epc->ebc/dot_general | solution.py:97
  62.0 1.8 fusion.104
  63.9 1.8 fusion.103
  67.5 3.1 %fusion.102 = bf16[8,1,1024,128]{3,2,1,0:T(8,128)(2,1)} fusion(bf16[8,1,1024,128]{3,2,1,0:T(8,128)(2,1)} %get-tuple-element.338, s32[]{:T(128)} %get-tuple-element.337, s32[4096]{0:T(1024)S(1)} %bitcast.206, s32[1024]{0:T(1024)S(1)} %iota_add_fusion.10, bf16[1,4096,128]{2,1,0:T(8,128)(2,1)S(1)} %get-tuple-element.355), kind=kOutput, calls=%fused_computation.21.clone.clone.1 | convolution fusion | flops 1078067200 | bytes 1331712 | tf_op jit(solution)/shard_map/while/body/eval_jaxpr/ebp,epc->ebc/dot_general | solution.py:97
  70.9 1.8 fusion.104
  72.7 1.8 fusion.103
  76.4 3.1 %fusion.102 = bf16[8,1,1024,128]{3,2,1,0:T(8,128)(2,1)} fusion(bf16[8,1,1024,128]{3,2,1,0:T(8,128)(2,1)} %get-tuple-element.338, s32[]{:T(128)} %get-tuple-element.337, s32[4096]{0:T(1024)S(1)} %bitcast.206, s32[1024]{0:T(1024)S(1)} %iota_add_fusion.10, bf16[1,4096,128]{2,1,0:T(8,128)(2,1)S(1)} %get-tuple-element.355), kind=kOutput, calls=%fused_computation.21.clone.clone.1 | convolution fusion | flops 1078067200 | bytes 1331712 | tf_op jit(solution)/shard_map/while/body/eval_jaxpr/ebp,epc->ebc/dot_general | solution.py:97
  79.7 1.8 fusion.104
  81.6 1.8 fusion.103
  85.2 3.1 %fusion.102 = bf16[8,1,1024,128]{3,2,1,0:T(8,128)(2,1)} fusion(bf16[8,1,1024,128]{3,2,1,0:T(8,128)(2,1)} %get-tuple-element.338, s32[]{:T(128)} %get-tuple-element.337, s32[4096]{0:T(1024)S(1)} %bitcast.206, s32[1024]{0:T(1024)S(1)} %iota_add_fusion.10, bf16[1,4096,128]{2,1,0:T(8,128)(2,1)S(1)} %get-tuple-element.355), kind=kOutput, calls=%fused_computation.21.clone.clone.1 | convolution fusion | flops 1078067200 | bytes 1331712 | tf_op jit(solution)/shard_map/while/body/eval_jaxpr/ebp,epc->ebc/dot_general | solution.py:97
  88.6 1.8 fusion.104
  90.4 1.8 fusion.103
  93.4 0.7 reduce.4
  94.1 16.2 %all_to_all.15 = bf16[32,2,128]{2,1,0:T(2,128)(2,1)S(1)} all-to-all(bf16[32,2,128]{2,1,0:T(2,128)(2,1)S(1)} %reshape.616), channel_id=1, replica_groups=mesh['expo'=4,'fp'=8] {'expo','fp'}, dimensions={0} | all-to-all | bytes 32768 | tf_op jit(solution)/shard_map/all_to_all | solution.py:125
  110.3 2.7 %all-to-all-start.2 = ((bf16[32,1,256,128]{3,2,1,0:T(8,128)(2,1)}), bf16[32,1,256,128]{3,2,1,0:T(8,128)(2,1)S(1)}, u32[]{:S(2)}, u32[]{:S(2)}) async-start(bf16[32,1,256,128]{3,2,1,0:T(8,128)(2,1)} %bitcast.189), calls=%async_computation.2 | async-start | bytes 4194304 | tf_op jit(solution)/shard_map/all_to_all | solution.py:123
  113.1 50.0 %all-to-all-done.2 = bf16[32,1,256,128]{3,2,1,0:T(8,128)(2,1)S(1)} async-done(((bf16[32,1,256,128]{3,2,1,0:T(8,128)(2,1)}), bf16[32,1,256,128]{3,2,1,0:T(8,128)(2,1)S(1)}, u32[]{:S(2)}, u32[]{:S(2)}) %all-to-all-start.2) | async-done | bytes 2097184 | tf_op jit(solution)/shard_map/all_to_all | solution.py:123
  163.1 2.8 %all-to-all-start = ((s32[32,1,256]{2,1,0:T(1,128)}), s32[32,1,256]{2,1,0:T(1,128)S(1)}, u32[]{:S(2)}, u32[]{:S(2)}) async-start(s32[32,1,256]{2,1,0:T(1,128)} %bitcast.46), calls=%async_computation | async-start | bytes 65536 | tf_op jit(solution)/shard_map/all_to_all | solution.py:124
  165.9 3.5 %fusion.26 = (bf16[8192,128]{1,0:T(8,128)(2,1)S(1)}, bf16[8192,128]{1,0:T(8,128)(2,1)S(1)}) fusion(bf16[32,1,256,128]{3,2,1,0:T(8,128)(2,1)S(1)} %all-to-all-done.2, f32[8192]{0:T(1024)S(1)} %bitcast.191), kind=kLoop, calls=%fused_computation.29 | loop fusion | flops 6291456 | bytes 6324224 | tf_op jit(solution)/shard_map/convert_element_type | solution.py:137
  169.4 2.4 pad_maximum_fusion
  171.7 1.1 all-to-all-done
  172.9 64.5 %while.28 = (s32[]{:T(128)}, f32[8,512,128]{2,1,0:T(8,128)S(1)}, f32[8,512]{1,0:T(8,128)S(1)}, s32[8]{0:T(128)S(1)}, s32[32,1,256]{2,1,0:T(1,128)S(1)}, /*index=...) while((s32[]{:T(128)}, f32[8,512,128]{2,1,0:T(8,128)S(1)}, ...), condition=%wide.region_9.10_spmd, body=%wide.region_7.9_spmd.sunk | while | flops 2164326400 | bytes 5615753 | solution.py:154
  174.1 4.6 %fusion.97 = f32[512,256]{1,0:T(8,128)S(1)} fusion(bf16[8192,256]{1,0:T(8,128)(2,1)} %get-tuple-element.386, s32[8192]{0:T(1024)S(1)} %bitcast.193, s32[512]{0:T(512)S(1)} %iota_add_fusion.9), kind=kOutput, calls=%fused_computation.2.clone.1 | convolution fusion | flops 2151677952 | bytes 4753408 | tf_op jit(solution)/shard_map/while/body/eval_jaxpr/dot_general | solution.py:145
  178.7 2.1 fusion.99
  182.2 4.6 %fusion.97 = f32[512,256]{1,0:T(8,128)S(1)} fusion(bf16[8192,256]{1,0:T(8,128)(2,1)} %get-tuple-element.386, s32[8192]{0:T(1024)S(1)} %bitcast.193, s32[512]{0:T(512)S(1)} %iota_add_fusion.9), kind=kOutput, calls=%fused_computation.2.clone.1 | convolution fusion | flops 2151677952 | bytes 4753408 | tf_op jit(solution)/shard_map/while/body/eval_jaxpr/dot_general | solution.py:145
  186.8 2.1 fusion.99
  190.3 4.6 %fusion.97 = f32[512,256]{1,0:T(8,128)S(1)} fusion(bf16[8192,256]{1,0:T(8,128)(2,1)} %get-tuple-element.386, s32[8192]{0:T(1024)S(1)} %bitcast.193, s32[512]{0:T(512)S(1)} %iota_add_fusion.9), kind=kOutput, calls=%fused_computation.2.clone.1 | convolution fusion | flops 2151677952 | bytes 4753408 | tf_op jit(solution)/shard_map/while/body/eval_jaxpr/dot_general | solution.py:145
  194.9 2.1 fusion.99
  198.3 4.6 %fusion.97 = f32[512,256]{1,0:T(8,128)S(1)} fusion(bf16[8192,256]{1,0:T(8,128)(2,1)} %get-tuple-element.386, s32[8192]{0:T(1024)S(1)} %bitcast.193, s32[512]{0:T(512)S(1)} %iota_add_fusion.9), kind=kOutput, calls=%fused_computation.2.clone.1 | convolution fusion | flops 2151677952 | bytes 4753408 | tf_op jit(solution)/shard_map/while/body/eval_jaxpr/dot_general | solution.py:145
  202.9 2.1 fusion.99
  206.4 4.6 %fusion.97 = f32[512,256]{1,0:T(8,128)S(1)} fusion(bf16[8192,256]{1,0:T(8,128)(2,1)} %get-tuple-element.386, s32[8192]{0:T(1024)S(1)} %bitcast.193, s32[512]{0:T(512)S(1)} %iota_add_fusion.9), kind=kOutput, calls=%fused_computation.2.clone.1 | convolution fusion | flops 2151677952 | bytes 4753408 | tf_op jit(solution)/shard_map/while/body/eval_jaxpr/dot_general | solution.py:145
  211.0 2.1 fusion.99
  214.4 4.6 %fusion.97 = f32[512,256]{1,0:T(8,128)S(1)} fusion(bf16[8192,256]{1,0:T(8,128)(2,1)} %get-tuple-element.386, s32[8192]{0:T(1024)S(1)} %bitcast.193, s32[512]{0:T(512)S(1)} %iota_add_fusion.9), kind=kOutput, calls=%fused_computation.2.clone.1 | convolution fusion | flops 2151677952 | bytes 4753408 | tf_op jit(solution)/shard_map/while/body/eval_jaxpr/dot_general | solution.py:145
  219.1 2.1 fusion.99
  222.5 4.6 %fusion.97 = f32[512,256]{1,0:T(8,128)S(1)} fusion(bf16[8192,256]{1,0:T(8,128)(2,1)} %get-tuple-element.386, s32[8192]{0:T(1024)S(1)} %bitcast.193, s32[512]{0:T(512)S(1)} %iota_add_fusion.9), kind=kOutput, calls=%fused_computation.2.clone.1 | convolution fusion | flops 2151677952 | bytes 4753408 | tf_op jit(solution)/shard_map/while/body/eval_jaxpr/dot_general | solution.py:145
  227.1 2.1 fusion.99
  230.6 4.6 %fusion.97 = f32[512,256]{1,0:T(8,128)S(1)} fusion(bf16[8192,256]{1,0:T(8,128)(2,1)} %get-tuple-element.386, s32[8192]{0:T(1024)S(1)} %bitcast.193, s32[512]{0:T(512)S(1)} %iota_add_fusion.9), kind=kOutput, calls=%fused_computation.2.clone.1 | convolution fusion | flops 2151677952 | bytes 4753408 | tf_op jit(solution)/shard_map/while/body/eval_jaxpr/dot_general | solution.py:145
  235.2 2.1 fusion.99
  237.4 0.6 copy.53
  238.0 1.7 bitcast_divide_fusion
  (142 shorter events, 23.4 us)
Async XLA Ops:
  0.6 7.0 %copy-start = (bf16[8,2,41]{2,1,0:T(2,128)(2,1)S(1)}, bf16[8,2,41]{2,1,0:T(2,128)(2,1)}, u32[]{:S(2)}) copy-start(bf16[8,2,41]{2,1,0:T(2,128)(2,1)} %param.12) | copy-start | bytes 3940
  1.6 16.5 %collective-permute-start = (bf16[1,20,2048]{2,1,0:T(8,128)(2,1)S(1)}, bf16[1,20,2048]{2,1,0:T(8,128)(2,1)S(1)}, u32[]{:S(2)}, u32[]{:S(2)}) collective-permute-start(bf16[1,20,2048]{2,1,0:T(8,128)(2,1)S(1)} %get-tuple-element.183), channel_id=1, source_target_pairs={{0,1},{1,2},{2,3},{3,4},{4,5},{5,6},{6,7},{8,9},{9,10},{10,11},{11... | collective-permute-start | bytes 245768 | tf_op jit(solution)/shard_map/ppermute | solution.py:18
  4.0 14.1 %collective-permute-start.1 = (bf16[1,20,2048]{2,1,0:T(8,128)(2,1)S(1)}, bf16[1,20,2048]{2,1,0:T(8,128)(2,1)S(1)}, u32[]{:S(2)}, u32[]{:S(2)}) collective-permute-start(bf16[1,20,2048]{2,1,0:T(8,128)(2,1)S(1)} %get-tuple-element.184), channel_id=1, source_target_pairs={{1,0},{2,1},{3,2},{4,3},{5,4},{6,5},{7,6},{9,8},{10,9},{11,10},{12... | collective-permute-start | bytes 245768 | tf_op jit(solution)/shard_map/ppermute | solution.py:19
  14.1 3.8 %copy-start.4 = (s32[1,256,16]{1,2,0:T(8,128)S(1)}, s32[1,256,16]{1,2,0:T(8,128)}, u32[]{:S(2)}) copy-start(s32[1,256,16]{1,2,0:T(8,128)} %param.17) | copy-start | bytes 49156
  14.1 4.0 %copy-start.2 = (bf16[1,256,2048]{2,1,0:T(8,128)(2,1)S(1)}, bf16[1,256,2048]{2,1,0:T(8,128)(2,1)}, u32[]{:S(2)}) copy-start(bf16[1,256,2048]{2,1,0:T(8,128)(2,1)} %param.11) | copy-start | bytes 3145732
  17.9 0.9 copy-start.3
  110.3 52.8 %all-to-all-start.2 = ((bf16[32,1,256,128]{3,2,1,0:T(8,128)(2,1)}), bf16[32,1,256,128]{3,2,1,0:T(8,128)(2,1)S(1)}, u32[]{:S(2)}, u32[]{:S(2)}) async-start(bf16[32,1,256,128]{3,2,1,0:T(8,128)(2,1)} %bitcast.189), calls=%async_computation.2 | async-start | bytes 4194304 | tf_op jit(solution)/shard_map/all_to_all | solution.py:123
  163.1 9.8 %all-to-all-start = ((s32[32,1,256]{2,1,0:T(1,128)}), s32[32,1,256]{2,1,0:T(1,128)S(1)}, u32[]{:S(2)}, u32[]{:S(2)}) async-start(s32[32,1,256]{2,1,0:T(1,128)} %bitcast.46), calls=%async_computation | async-start | bytes 65536 | tf_op jit(solution)/shard_map/all_to_all | solution.py:124
  169.4 3.5 %copy-start.1 = (f32[8,512,128]{2,1,0:T(8,128)S(1)}, f32[8,512,128]{2,1,0:T(8,128)}, u32[]{:S(2)}) copy-start(f32[8,512,128]{2,1,0:T(8,128)} %custom-call) | copy-start | bytes 6291460
where the time goes:
time: 241 us; the launch traced here: 240 us
  matrix products  69.3 us (29%)
  other arithmetic  58.7 us (24%)
  waiting for transfers between devices  51.1 us (21%)
  local copies, waits for them, and re-layouts  21.2 us (9%)
  blocking collectives  16.2 us (7%)
  loops' own time  11 us (5%)
  starting transfers between devices  9.19 us (4%)
  between operations  3.03 us (1%)
    all_to_all x1, waiting for transfers between devices, body(): lax.all_to_all(send_values, ('expo', 'fp'), split_axis=0, concat_axis=0,...  50 us
    dot_general x8, matrix products, sum_block(): jnp.dot(matched.astype(jnp.bfloat16), both_parts, preferred_element_type=...  36.5 us
    dot_general x8, matrix products, pack_block(): jnp.einsum('ebp,epc->ebc', matched.astype(jnp.bfloat16), convolved, prefe...  24.9 us
    reduce_sum x8, other arithmetic, sum_block(): jnp.sum(jnp.where(matched, flat_weights[None, :], jnp.zeros((), jnp.float...  16.9 us
    all_to_all x1, blocking collectives, body(): lax.all_to_all(send_weights.astype(jnp.bfloat16), ('expo', 'fp'), split_a...  16.2 us
    reduce_sum x8, other arithmetic, pack_block(): jnp.sum(jnp.where(matched, piece_weight[:, None, :], jnp.zeros((), jnp.fl...  14.7 us
    reduce_sum x8, other arithmetic, pack_block(): slot_offsets = jnp.sum(jnp.where(matched, offsets[:, None, :], 0), axis=2)  14.7 us
    dynamic_slice x16, local copies, waits for them, and re-layouts, body(): lax.map(pack_block, jnp.arange(send_slots // send_block))  9.41 us
  transfers between devices with their start and end apart: 4, of which 2 were waited for; matrix products, arithmetic and copies ran while one was open for 7% of the time, Pallas kernels for 0%

commit v1 on v0

v1 whole, which is shorter than its diff:
```python
import functools

import jax
import jax.numpy as jnp
from jax import lax
from jax.experimental import pallas as pl
from jax.experimental.pallas import tpu as pltpu
from jax.sharding import PartitionSpec as P

GAP = 32
EDGE = 32
LANES = 128
SPLIT = 4

VMEM = pl.BlockSpec(memory_space=pltpu.VMEM)
SMEM = pl.BlockSpec(memory_space=pltpu.SMEM)
ANY = pl.BlockSpec(memory_space=pl.ANY)


def iota(shape, dim):
    return lax.broadcasted_iota(jnp.int32, shape, dim)


def dot_last(a, b):
    return lax.dot_general(a, b, (((1,), (1,)), ((), ())), preferred_element_type=jnp.float32)


def halo(shard, axis):
    size = lax.axis_size(axis)
    up = [(i, i + 1) for i in range(size - 1)]
    down = [(i + 1, i) for i in range(size - 1)]
    above = lax.ppermute(shard[-EDGE:], axis, up)
    below = lax.ppermute(shard[:EDGE], axis, down)
    return above, below


def route_kernel(half, tile_ref, off_ref, gap_ref, var_ref, id_ref, bank_ref, dest_ref, meta_ref, tv_ref, th_ref):
    segs, rows = off_ref.shape
    devices = meta_ref.shape[0]
    capacity = meta_ref.shape[1] - LANES
    taps = bank_ref[id_ref[0, 0]]
    for ref, which, shift in ((tv_ref, 0, EDGE - half), (th_ref, 1, LANES - half)):
        height, width = ref.shape
        line = jnp.concatenate([taps[which : which + 1, :]] + [jnp.zeros((1, LANES), jnp.float32)] * (width // LANES - 1), axis=1)
        wide = jnp.broadcast_to(line, (height, width))
        ref[...] = pltpu.roll(wide, shift // 8 * 8, 1, stride=1, stride_axis=0).astype(jnp.bfloat16)
    gap = gap_ref[0, 0]
    line = iota((1, rows), 1)
    kept = jnp.logical_or(line < gap, line >= gap + GAP)
    before = (iota((rows, rows), 0) < iota((rows, rows), 1)).astype(jnp.bfloat16)
    owner = iota((devices, rows), 0)
    place = iota((capacity, rows), 0)
    base = jnp.zeros((devices, 1), jnp.float32)
    packed = jnp.zeros((3 * devices, capacity), jnp.float32)
    for s in range(segs):
        tile = jnp.where(kept, tile_ref[s], -1)
        hot = tile == owner
        hot_value = hot.astype(jnp.float32)
        hot_low = hot_value.astype(jnp.bfloat16)
        prefix = jnp.dot(hot_low, before, preferred_element_type=jnp.float32)
        rank = jnp.sum(hot_value * (prefix + base), axis=0, keepdims=True).astype(jnp.int32)
        base = base + jnp.sum(hot_value, axis=1, keepdims=True)
        dest_ref[s : s + 1, :] = jnp.where(kept, tile * capacity + rank, devices * capacity)
        spot = (place == rank).astype(jnp.bfloat16)
        offset = off_ref[s : s + 1, :]
        high = (offset >> 6).astype(jnp.float32)
        low = (offset & 63).astype(jnp.float32)
        stack = jnp.concatenate([hot_value * high, hot_value * low, hot_value], axis=0).astype(jnp.bfloat16)
        packed = packed + dot_last(stack, spot)
    found = packed[2 * devices :] > 0.5
    offsets = packed[:devices] * 64.0 + packed[devices : 2 * devices]
    meta_ref[:, :capacity] = jnp.where(found, offsets, -1.0)
    meta_ref[:, capacity:] = jnp.full((devices, LANES), var_ref[0, 0], jnp.float32)


def pack_kernel(raw_ref, above_ref, below_ref, tv_ref, th_ref, dest_ref, out_ref, edged, vert, conv, spread, sems):
    rows, cols = raw_ref.shape
    segs = cols // LANES
    copies = [
        pltpu.make_async_copy(above_ref, edged.at[pl.ds(0, EDGE)], sems.at[0]),
        pltpu.make_async_copy(raw_ref, edged.at[pl.ds(EDGE, rows)], sems.at[1]),
        pltpu.make_async_copy(below_ref, edged.at[pl.ds(EDGE + rows, EDGE)], sems.at[2]),
    ]
    for copy in copies:
        copy.start()
    vert[:, :LANES] = jnp.zeros((rows, LANES), jnp.bfloat16)
    vert[:, LANES + cols :] = jnp.zeros((rows, LANES), jnp.bfloat16)
    for copy in copies:
        copy.wait()
    wide = 2 * LANES
    tall = rows + 2 * EDGE
    for c in range(cols // wide):
        part = jnp.dot(tv_ref[:, :tall], edged[:, c * wide : (c + 1) * wide], preferred_element_type=jnp.float32)
        vert[:, LANES + c * wide : LANES + (c + 1) * wide] = part.astype(jnp.bfloat16)
    for c in range(cols // wide):
        part = dot_last(vert[:, c * wide : c * wide + 2 * wide], th_ref[...])
        conv[2 * c * rows : (2 * c + 1) * rows, :] = part[:, :LANES]
        conv[(2 * c + 1) * rows : (2 * c + 2) * rows, :] = part[:, LANES:]

    group = 32

    def scatter(step, carry):
        start = pl.multiple_of(step * group, group)
        for j in range(group):
            spot = dest_ref[start + j]
            spread[pl.ds(spot, 1), :] = conv[pl.ds(start + j, 1), :]
        return carry

    lax.fori_loop(0, segs * rows // group, scatter, 0)

    devices, capacity, _ = out_ref.shape

    def emit(step, carry):
        start = pl.multiple_of(step * capacity, capacity)
        out_ref[step] = spread[pl.ds(start, capacity), :].astype(jnp.bfloat16)
        return carry

    lax.fori_loop(0, devices, emit, 0)


def sum_kernel(values_ref, meta_ref, off_ref, var_ref, image_ref, weight_ref, scaled, *sums):
    devices, capacity, _ = values_ref.shape
    slots = image_ref.shape[0]
    high_rows = slots // LANES

    def clear(step, carry):
        start = pl.multiple_of(step * 64, 64)
        for acc in sums:
            acc[pl.ds(start, 64), :] = jnp.zeros((64, LANES), jnp.float32)
        return carry

    lax.fori_loop(0, slots // 64, clear, 0)

    high_id = iota((high_rows, capacity), 0)
    low_id = iota((LANES, capacity), 0)

    def source(src, weight):
        factor = var_ref[src]
        scaled[...] = values_ref[src].astype(jnp.float32) * factor
        offset = meta_ref[src, :, :capacity].astype(jnp.int32)
        high = ((offset >> 7) == high_id).astype(jnp.bfloat16)
        low = ((offset & 127) == low_id).astype(jnp.bfloat16)
        count = dot_last(high, low)

        group = 32

        def add(step, carry):
            start = pl.multiple_of(step * group, group)
            for j in range(0, group, len(sums)):
                spots = [off_ref[src * capacity + start + j + k] for k in range(len(sums))]
                held = [acc[pl.ds(spot, 1), :] for acc, spot in zip(sums, spots)]
                fresh = [scaled[pl.ds(start + j + k, 1), :] for k in range(len(sums))]
                for acc, spot, one, two in zip(sums, spots, held, fresh):
                    acc[pl.ds(spot, 1), :] = one + two
            return carry

        lax.fori_loop(0, capacity // group, add, 0)
        return weight + factor * count

    weight = lax.fori_loop(0, devices, source, jnp.zeros((high_rows, LANES), jnp.float32))
    weight_ref[...] = weight
    for h in range(high_rows):
        scale = jnp.broadcast_to(jnp.maximum(weight[h : h + 1, :], 1.0), (LANES, LANES)).T
        total = sums[0][h * LANES : (h + 1) * LANES, :]
        for acc in sums[1:]:
            total = total + acc[h * LANES : (h + 1) * LANES, :]
        image_ref[h * LANES : (h + 1) * LANES, :] = total / scale


def body(raw_pixels, kernel_bank, kernel_ids, inv_var, gap_start, warp_tile, warp_offset):
    _, rows, cols = raw_pixels.shape
    segs = cols // LANES
    axes = ("expo", "fp")
    devices = lax.axis_size("expo") * lax.axis_size("fp")
    pieces = rows * segs
    capacity = 2 * pieces // devices
    slots = pieces
    f32, bf16, i32 = jnp.float32, jnp.bfloat16, jnp.int32

    raw = raw_pixels[0]
    above, below = halo(raw, "fp")
    tiles = jnp.transpose(warp_tile[0], (1, 2, 0))
    offsets = jnp.transpose(warp_offset[0], (1, 0))
    taps = kernel_bank.shape[2]
    lead = -(taps // 2) % 8
    bank = jnp.pad(kernel_bank.astype(f32), ((0, 0), (0, 0), (lead, LANES - taps - lead)))
    tall = -(-(rows + 2 * EDGE) // LANES) * LANES
    dest, meta, tv, th = pl.pallas_call(
        functools.partial(route_kernel, taps // 2),
        out_shape=(
            jax.ShapeDtypeStruct((segs, rows), i32),
            jax.ShapeDtypeStruct((devices, capacity + LANES), f32),
            jax.ShapeDtypeStruct((rows, tall), bf16),
            jax.ShapeDtypeStruct((2 * LANES, 4 * LANES), bf16),
        ),
        in_specs=[VMEM, VMEM, SMEM, SMEM, SMEM, VMEM],
        out_specs=(VMEM, VMEM, VMEM, VMEM),
        cost_estimate=pl.CostEstimate(flops=400_000_000, bytes_accessed=600_000, transcendentals=0),
        name="route",
    )(tiles, offsets, gap_start, inv_var, kernel_ids, bank)

    got_meta = lax.all_to_all(meta, axes, split_axis=0, concat_axis=0, tiled=True)

    send = pl.pallas_call(
        pack_kernel,
        out_shape=jax.ShapeDtypeStruct((devices, capacity, LANES), bf16),
        in_specs=[ANY, ANY, ANY, VMEM, VMEM, SMEM],
        out_specs=VMEM,
        scratch_shapes=[
            pltpu.VMEM((rows + 2 * EDGE, cols), bf16),
            pltpu.VMEM((rows, cols + 2 * LANES), bf16),
            pltpu.VMEM((pieces, LANES), f32),
            pltpu.VMEM((devices * capacity + 8, LANES), f32),
            pltpu.SemaphoreType.DMA((3,)),
        ],
        cost_estimate=pl.CostEstimate(flops=10_000_000_000, bytes_accessed=4_000_000, transcendentals=0),
        name="pack",
    )(raw, above, below, tv, th, dest.reshape(-1))

    got = lax.all_to_all(send, axes, split_axis=0, concat_axis=0, tiled=True)

    spots = got_meta[:, :capacity].astype(i32)
    spots = jnp.where(spots < 0, slots, spots).reshape(-1)
    factors = got_meta[:, capacity]
    image, weight = pl.pallas_call(
        sum_kernel,
        out_shape=(
            jax.ShapeDtypeStruct((slots, LANES), f32),
            jax.ShapeDtypeStruct((slots // LANES, LANES), f32),
        ),
        in_specs=[VMEM, VMEM, SMEM, SMEM],
        out_specs=(VMEM, VMEM),
        scratch_shapes=[pltpu.VMEM((capacity, LANES), f32)]
        + [pltpu.VMEM((slots + 8, LANES), f32) for _ in range(SPLIT)],
        cost_estimate=pl.CostEstimate(flops=10_000_000_000, bytes_accessed=4_000_000, transcendentals=0),
        name="sum",
    )(got, got_meta.reshape(devices, 1, -1), spots, factors)
    return image[None], weight.reshape(1, slots)


def solution(mesh):
    in_specs = (
        P("expo", "fp", None),
        P(),
        P("expo", "fp"),
        P("expo", "fp"),
        P("expo", "fp"),
        P("expo", "fp", None, None),
        P("expo", "fp", None),
    )
    out_specs = (P(("expo", "fp"), None, None), P(("expo", "fp"), None))
    return jax.shard_map(body, mesh=mesh, in_specs=in_specs, out_specs=out_specs, check_vma=False)
```

time: 241 us -> 112 us (0.46)
  matrix products: 69.3 us -> 0 us
  other arithmetic: 58.7 us -> 1.37 us
  Pallas kernels: 0 us -> 33.3 us
  blocking collectives: 16.2 us -> 0 us
  local copies, waits for them, and re-layouts: 21.2 us -> 7.03 us
  loops' own time: 11 us -> 0 us
  starting transfers between devices: 9.19 us -> 17.5 us
    dot_general x28 -> x0, matrix products: 69.3 us -> none  [the longest x8 36.5 us: sum_block(): jnp.dot(matched.astype(jnp.bfloat16), both_parts, preferred_element_type=...]
    reduce_sum x25 -> x0, other arithmetic: 46.6 us -> none  [the longest x8 16.9 us: sum_block(): jnp.sum(jnp.where(matched, flat_weights[None, :], jnp.zeros((), jnp.float...]
    pallas_call x0 -> x3, Pallas kernels: none -> 33.3 us  [the longest x1 20.8 us: body(): pl.pallas_call(sum_kernel, out_shape=(jax.ShapeDtypeStruct((slots, LANES)...]
    all_to_all x1 -> x0, blocking collectives: 16.2 us -> none  [body(): lax.all_to_all(send_weights.astype(jnp.bfloat16), ('expo', 'fp'), split_a...]
    another operation x2 -> x0, loops' own time: 11 us -> none  [the longest x1 5.57 us: body(): lax.map(sum_block, jnp.arange(pieces // sum_block_rows))]
    dynamic_slice x16 -> x0, local copies, waits for them, and re-layouts: 9.41 us -> none  [body(): lax.map(pack_block, jnp.arange(send_slots // send_block))]
    all_to_all x2, starting transfers between devices: 5.49 us -> 13.2 us  [the longest x1 7.32 us: body(): lax.all_to_all(meta, axes, split_axis=0, concat_axis=0, tiled=True)]
    dynamic_update_slice x24 -> x0, local copies, waits for them, and re-layouts: 5.37 us -> none  [the longest x16 4.9 us: body(): lax.map(pack_block, jnp.arange(send_slots // send_block))]
  transfers between devices with their start and end apart: 4 -> 4, of which waited for: 2 -> 1; matrix products, arithmetic and copies ran while one was open for 7% -> 4% of each run, Pallas kernels for 0% -> 11%
where the time goes in v1:
time: 112 us; the launch traced here: 111 us
  waiting for transfers between devices  48.8 us (44%)
  Pallas kernels  33.3 us (30%)
  starting transfers between devices  17.5 us (16%)
  local copies, waits for them, and re-layouts  7.03 us (6%)
  between operations  2.67 us (2%)
  other arithmetic  1.37 us (1%)
    all_to_all x1, waiting for transfers between devices, body(): got = lax.all_to_all(send, axes, split_axis=0, concat_axis=0, tiled=True)  48.7 us
    pallas_call x1, Pallas kernels, body(): pl.pallas_call(sum_kernel, out_shape=(jax.ShapeDtypeStruct((slots, LANES)...  20.8 us
    pallas_call x1, Pallas kernels, body(): pl.pallas_call(pack_kernel, out_shape=jax.ShapeDtypeStruct((devices, capa...  9.13 us
    all_to_all x1, starting transfers between devices, body(): lax.all_to_all(meta, axes, split_axis=0, concat_axis=0, tiled=True)  7.32 us
    all_to_all x1, starting transfers between devices, body(): got = lax.all_to_all(send, axes, split_axis=0, concat_axis=0, tiled=True)  5.84 us
    unnamed x11, local copies, waits for them, and re-layouts  3.99 us
    pallas_call x1, Pallas kernels, body(): pl.pallas_call(functools.partial(route_kernel, taps // 2), out_shape=(jax...  3.45 us
    ppermute x1, starting transfers between devices, halo(): above = lax.ppermute(shard[-EDGE:], axis, up)  3.04 us
  transfers between devices with their start and end apart: 4, of which 1 were waited for; matrix products, arithmetic and copies ran while one was open for 4% of the time, Pallas kernels for 11%

profile of v1, /device:TPU:0, one launch (start us, length us, event | category | flops | bytes accessed | tf_op | source)
XLA Modules:
  0.0 110.7 jit_solution(6660447873814966910)
XLA Ops:
  0.6 1.0 slice_bitcast_fusion
  1.6 1.3 %collective-permute-start.1 = (bf16[32,2048]{1,0:T(8,128)(2,1)S(1)}, bf16[32,2048]{1,0:T(8,128)(2,1)S(1)}, u32[]{:S(2)}, u32[]{:S(2)}) collective-permute-start(bf16[32,2048]{1,0:T(8,128)(2,1)S(1)} %get-tuple-element.14), channel_id=1, source_target_pairs={{1,0},{2,1},{3,2},{4,3},{5,4},{6,5},{7,6},{9,8},{10,9},{11,10},{12... | collective-permute-start | bytes 393224 | tf_op jit(solution)/shard_map/ppermute | solution.py:33
  2.9 3.0 %collective-permute-start = (bf16[32,2048]{1,0:T(8,128)(2,1)S(1)}, bf16[32,2048]{1,0:T(8,128)(2,1)S(1)}, u32[]{:S(2)}, u32[]{:S(2)}) collective-permute-start(bf16[32,2048]{1,0:T(8,128)(2,1)S(1)} %get-tuple-element.15), channel_id=1, source_target_pairs={{0,1},{1,2},{2,3},{3,4},{4,5},{5,6},{6,7},{8,9},{9,10},{10,11},{11... | collective-permute-start | bytes 393224 | tf_op jit(solution)/shard_map/ppermute | solution.py:32
  7.9 1.4 %pad_convert_fusion.bank_ref = f32[8,2,128]{2,1,0:T(2,128)} fusion(bf16[8,2,41]{2,1,0:T(2,128)(2,1)} %param.8), kind=kLoop, calls=%fused_computation.7 | loop fusion | flops 2048 | bytes 9504 | tf_op jit(solution)/shard_map/jit(_pad)/pad | solution.py:186
  9.3 3.4 %route.1 = (s32[16,256]{1,0:T(8,128)}, f32[32,384]{1,0:T(8,128)}, bf16[256,384]{1,0:T(8,128)(2,1)}, bf16[256,512]{1,0:T(8,128)(2,1)}) custom-call(s32[16,1,256]{2,1,0:T(1,128)} %bitcast.27, s32[16,256]{1,0:T(8,128)} %bitcast.28, s32[1,1]{1,0:T(1,128)S(6)} %copy.16.gap_ref, f32[1,1]{1,0:T(1,128)S(6)} %copy.15.var_ref, s32[1,1]{1,0:T(1,128)S(6)} %copy.14.id_ref, ...), custom_call_target="tpu_custom_call" | custom-call | flops 400000000 | bytes 600000 | tf_op jit(solution)/shard_map/route/pallas_call | solution.py:188
  12.7 1.4 %all_to_all.12 = f32[32,1,384]{2,1,0:T(1,128)} reshape(f32[32,384]{1,0:T(8,128)} %get-tuple-element.11) | data formatting | bytes 98304 | tf_op jit(solution)/shard_map/all_to_all | solution.py:202
  14.2 7.3 %all-to-all-start.1 = ((f32[32,1,384]{2,1,0:T(1,128)}), f32[32,1,384]{2,1,0:T(1,128)S(1)}, u32[]{:S(2)}, u32[]{:S(2)}) async-start(f32[32,1,384]{2,1,0:T(1,128)} %all_to_all.12), calls=%async_computation.1 | async-start | bytes 98304 | tf_op jit(solution)/shard_map/all_to_all | solution.py:202
  21.5 1.3 %copy.10 = s32[2,2,8,128]{3,1,2,0:T(2,128)} copy(s32[2,2,8,128]{3,2,1,0:T(8,128)} %bitcast.25) | data formatting | bytes 32768
  22.8 0.0 collective-permute-done.1.below_ref
  22.8 0.0 copy-start.2
  22.8 0.0 collective-permute-done.above_ref
  22.8 0.0 copy-start.3
  22.8 0.6 copy-done.2
  23.5 0.1 copy-done.3
  23.5 9.1 %pack.1 = bf16[32,256,128]{2,1,0:T(8,128)(2,1)} custom-call(bf16[256,2048]{1,0:T(8,128)(2,1)} %bitcast.23, bf16[32,2048]{1,0:T(8,128)(2,1)} %copy-done.3, bf16[32,2048]{1,0:T(8,128)(2,1)} %copy-done.2, bf16[256,384]{1,0:T(8,128)(2,1)} %get-tuple-element.8.tv_ref, bf16[256,512]{1,0:T(8,128)(2,1)} %get-tuple-element.9.th_ref, s32[4096]{0:T(1024)} %bitcast.26), custom_call_target="tpu_custom_call" | custom-call | flops 10000000000 | bytes 4000000 | tf_op jit(solution)/shard_map/pack/pallas_call | solution.py:204
  32.7 0.0 all-to-all-done.1.meta_ref
  32.7 0.0 copy-start.1
  32.7 5.8 %all-to-all-start = ((bf16[32,256,128]{2,1,0:T(8,128)(2,1)}), bf16[32,256,128]{2,1,0:T(8,128)(2,1)S(1)}, u32[]{:S(2)}, u32[]{:S(2)}) async-start(bf16[32,256,128]{2,1,0:T(8,128)(2,1)} %pack.1), calls=%async_computation | async-start | bytes 4194304 | tf_op jit(solution)/shard_map/all_to_all | solution.py:220
  38.5 0.0 copy-done.1
  38.6 0.6 copy.11
  39.2 0.6 slice_reduce_fusion.var_ref
  39.8 48.7 %all-to-all-done.values_ref = bf16[32,256,128]{2,1,0:T(8,128)(2,1)S(1)} async-done(((bf16[32,256,128]{2,1,0:T(8,128)(2,1)}), bf16[32,256,128]{2,1,0:T(8,128)(2,1)S(1)}, u32[]{:S(2)}, u32[]{:S(2)}) %all-to-all-start) | async-done | bytes 2097184 | tf_op jit(solution)/shard_map/all_to_all | solution.py:220
  88.6 0.0 copy-start
  88.6 1.3 %copy-done = bf16[32,256,128]{2,1,0:T(8,128)(2,1)} copy-done((bf16[32,256,128]{2,1,0:T(8,128)(2,1)}, bf16[32,256,128]{2,1,0:T(8,128)(2,1)S(1)}, u32[]{:S(2)}) %copy-start) | copy-done | bytes 2097176
  89.9 20.8 %sum.1 = (f32[4096,128]{1,0:T(8,128)}, f32[32,128]{1,0:T(8,128)}) custom-call(bf16[32,256,128]{2,1,0:T(8,128)(2,1)} %copy-done, f32[32,1,384]{2,1,0:T(1,128)} %copy-done.1, s32[8192]{0:T(1024)} %bitcast.24, f32[32]{0:T(128)} %slice_reduce_fusion.var_ref), custom_call_target="tpu_custom_call" | custom-call | flops 10000000000 | bytes 4000000 | tf_op jit(solution)/shard_map/sum/pallas_call | solution.py:225
  (2 shorter events, 0.0 us)
Async XLA Ops:
  1.6 21.2 %collective-permute-start.1 = (bf16[32,2048]{1,0:T(8,128)(2,1)S(1)}, bf16[32,2048]{1,0:T(8,128)(2,1)S(1)}, u32[]{:S(2)}, u32[]{:S(2)}) collective-permute-start(bf16[32,2048]{1,0:T(8,128)(2,1)S(1)} %get-tuple-element.14), channel_id=1, source_target_pairs={{1,0},{2,1},{3,2},{4,3},{5,4},{6,5},{7,6},{9,8},{10,9},{11,10},{12... | collective-permute-start | bytes 393224 | tf_op jit(solution)/shard_map/ppermute | solution.py:33
  2.9 19.9 %collective-permute-start = (bf16[32,2048]{1,0:T(8,128)(2,1)S(1)}, bf16[32,2048]{1,0:T(8,128)(2,1)S(1)}, u32[]{:S(2)}, u32[]{:S(2)}) collective-permute-start(bf16[32,2048]{1,0:T(8,128)(2,1)S(1)} %get-tuple-element.15), channel_id=1, source_target_pairs={{0,1},{1,2},{2,3},{3,4},{4,5},{5,6},{6,7},{8,9},{9,10},{10,11},{11... | collective-permute-start | bytes 393224 | tf_op jit(solution)/shard_map/ppermute | solution.py:32
  14.2 18.5 %all-to-all-start.1 = ((f32[32,1,384]{2,1,0:T(1,128)}), f32[32,1,384]{2,1,0:T(1,128)S(1)}, u32[]{:S(2)}, u32[]{:S(2)}) async-start(f32[32,1,384]{2,1,0:T(1,128)} %all_to_all.12), calls=%async_computation.1 | async-start | bytes 98304 | tf_op jit(solution)/shard_map/all_to_all | solution.py:202
  22.8 0.7 copy-start.2
  22.8 0.7 copy-start.3
  32.7 5.9 %copy-start.1 = (f32[32,1,384]{2,1,0:T(1,128)}, f32[32,1,384]{2,1,0:T(1,128)S(1)}, u32[]{:S(2)}) copy-start(f32[32,1,384]{2,1,0:T(1,128)S(1)} %all-to-all-done.1.meta_ref) | copy-start | bytes 147460
  32.7 55.9 %all-to-all-start = ((bf16[32,256,128]{2,1,0:T(8,128)(2,1)}), bf16[32,256,128]{2,1,0:T(8,128)(2,1)S(1)}, u32[]{:S(2)}, u32[]{:S(2)}) async-start(bf16[32,256,128]{2,1,0:T(8,128)(2,1)} %pack.1), calls=%async_computation | async-start | bytes 4194304 | tf_op jit(solution)/shard_map/all_to_all | solution.py:220
  88.6 1.3 %copy-start = (bf16[32,256,128]{2,1,0:T(8,128)(2,1)}, bf16[32,256,128]{2,1,0:T(8,128)(2,1)S(1)}, u32[]{:S(2)}) copy-start(bf16[32,256,128]{2,1,0:T(8,128)(2,1)S(1)} %all-to-all-done.values_ref) | copy-start | bytes 6291460

commit v2 on v1

v2 whole, which is shorter than its diff:
```python
import functools

import jax
import jax.numpy as jnp
from jax import lax
from jax.experimental import pallas as pl
from jax.experimental.pallas import tpu as pltpu
from jax.sharding import PartitionSpec as P

GAP = 32
EDGE = 32
LANES = 128
META = 8
SPLIT = (8, 4)
GROUP = 8

VMEM = pl.BlockSpec(memory_space=pltpu.VMEM)
ANY = pl.BlockSpec(memory_space=pl.ANY)
f32, bf16, i32 = jnp.float32, jnp.bfloat16, jnp.int32


def iota(shape, dim):
    return lax.broadcasted_iota(i32, shape, dim)


def dot_last(a, b):
    return lax.dot_general(a, b, (((1,), (1,)), ((), ())), preferred_element_type=f32)


def near(x):
    return pltpu.with_memory_space_constraint(x, pltpu.VMEM)


def far(x):
    return pltpu.with_memory_space_constraint(x, pltpu.HBM)


def params(mib):
    return pltpu.CompilerParams(vmem_limit_bytes=mib << 20)


def cost(flops, moved):
    return pl.CostEstimate(flops=flops, bytes_accessed=moved, transcendentals=0)


def halo(shard, axis):
    size = lax.axis_size(axis)
    up = [(i, i + 1) for i in range(size - 1)]
    down = [(i + 1, i) for i in range(size - 1)]
    above = lax.ppermute(shard[-EDGE:], axis, up)
    below = lax.ppermute(shard[:EDGE], axis, down)
    return above, below


def route_kernel(capacity, tile_ref, off_ref, gap_ref, var_ref, id_ref, bank_ref, dest_ref, meta_ref, tv_ref, th_ref, line_ref):
    segs, rows = off_ref.shape
    devices = meta_ref.shape[0] // META
    parts = -(-capacity // LANES)
    bank = bank_ref[...].astype(f32)
    chosen = jnp.where(id_ref[...] == 0, bank[0], 0.0)
    for k in range(1, bank.shape[0]):
        chosen = jnp.where(id_ref[...] == k, bank[k], chosen)
    taps = bank.shape[2]
    half = taps // 2
    lead = -half % 8
    line_ref[...] = jnp.zeros(line_ref.shape, f32)
    line_ref[:, lead : lead + taps] = chosen
    for ref, which, shift in ((tv_ref, 0, EDGE - half), (th_ref, 1, LANES - half)):
        height, width = ref.shape
        wide = jnp.broadcast_to(line_ref[which : which + 1, :width], (height, width))
        ref[...] = pltpu.roll(wide, shift - lead, 1, stride=1, stride_axis=0).astype(bf16)
    gap = gap_ref[...]
    line = iota((1, rows), 1)
    kept = jnp.logical_or(line < gap, line >= gap + GAP)
    before = (iota((rows, rows), 0) < iota((rows, rows), 1)).astype(bf16)
    owner = iota((devices, rows), 0)
    owner8 = iota((devices * META, rows), 0) >> 3
    field = iota((META, rows), 0)
    place = iota((LANES, rows), 0)
    base = jnp.zeros((devices, 1), f32)
    packed = jnp.zeros((devices * META, LANES), f32)
    for s in range(segs):
        tile = jnp.where(kept, tile_ref[s], -1)
        hot = (tile == owner).astype(f32)
        prefix = jnp.dot(hot.astype(bf16), before, preferred_element_type=f32)
        rank = jnp.sum(hot * (prefix + base), axis=0, keepdims=True).astype(i32)
        base = base + jnp.sum(hot, axis=1, keepdims=True)
        dest = jnp.where(kept, tile * capacity + rank, devices * capacity)
        for h in range(rows // LANES):
            dest_ref[s * (rows // LANES) + h] = dest[:, h * LANES : (h + 1) * LANES]
        offset = off_ref[s : s + 1, :]
        part = rank >> 7
        value = jnp.where(field == part, (offset >> 6) + 1, 0)
        value = jnp.where(field == part + parts, offset & 63, value).astype(f32)
        spread = jnp.concatenate([value] * devices, axis=0)
        stack = jnp.where(tile == owner8, spread, 0.0).astype(bf16)
        spot = (place == (rank & (LANES - 1))).astype(bf16)
        packed = packed + dot_last(stack, spot)
    var = var_ref[...]
    first = var.astype(bf16).astype(f32)
    second = (var - first).astype(bf16).astype(f32)
    third = var - first - second
    row = iota((devices * META, LANES), 0) & (META - 1)
    packed = jnp.where(row == 4, first, packed)
    packed = jnp.where(row == 5, second, packed)
    packed = jnp.where(row == 6, third, packed)
    meta_ref[...] = packed.astype(bf16)


def pack_kernel(raw_ref, above_ref, below_ref, tv_ref, th_ref, dest_ref, meta_ref, out0_ref, out1_ref, edged, vert, conv, spread, sems, *tables):
    rows, cols = raw_ref.shape
    copies = [
        pltpu.make_async_copy(above_ref, edged.at[pl.ds(0, EDGE)], sems.at[0]),
        pltpu.make_async_copy(raw_ref, edged.at[pl.ds(EDGE, rows)], sems.at[1]),
        pltpu.make_async_copy(below_ref, edged.at[pl.ds(EDGE + rows, EDGE)], sems.at[2]),
    ]
    for k, table in enumerate(tables):
        copies.append(pltpu.make_async_copy(dest_ref.at[pl.ds(k, 1)], table, sems.at[3 + k]))
    for copy in copies:
        copy.start()
    vert[:, :LANES] = jnp.zeros((rows, LANES), bf16)
    vert[:, LANES + cols :] = jnp.zeros((rows, LANES), bf16)
    devices, extended, _ = out0_ref.shape
    capacity0 = extended - META
    capacity1 = out1_ref.shape[1]
    out0_ref[:, capacity0:, :] = meta_ref[...].reshape(devices, META, LANES)
    for copy in copies:
        copy.wait()
    wide = 2 * LANES
    tall = rows + 2 * EDGE
    for c in range(cols // wide):
        part = jnp.dot(tv_ref[:, :tall], edged[:, c * wide : (c + 1) * wide], preferred_element_type=f32)
        vert[:, LANES + c * wide : LANES + (c + 1) * wide] = part.astype(bf16)
    for c in range(cols // wide):
        part = dot_last(vert[:, c * wide : c * wide + 2 * wide], th_ref[...])
        conv[2 * c * rows : (2 * c + 1) * rows, :] = part[:, :LANES]
        conv[(2 * c + 1) * rows : (2 * c + 2) * rows, :] = part[:, LANES:]

    def scatter(r, carry):
        for k, table in enumerate(tables):
            spread[pl.ds(table[0, 0, r], 1), :] = conv[pl.ds(r + k * LANES, 1), :]
        return carry

    lax.fori_loop(0, LANES, scatter, 0, unroll=2)

    capacity = capacity0 + capacity1

    def emit(step, carry):
        start = pl.multiple_of(step * capacity, capacity)
        out0_ref[step, :capacity0, :] = spread[pl.ds(start, capacity0), :].astype(bf16)
        out1_ref[step] = spread[pl.ds(start + capacity0, capacity1), :].astype(bf16)
        return carry

    lax.fori_loop(0, devices, emit, 0)


def clear_all(sums, slots):
    def clear(step, carry):
        block = pl.ds(pl.multiple_of(step * 64, 64), 64)
        for acc in sums:
            acc[block, :] = jnp.zeros((64, LANES), f32)
        return carry

    lax.fori_loop(0, slots // 64, clear, 0)


def merged(values):
    while len(values) > 1:
        values = [a + b for a, b in zip(values[::2], values[1::2])] + values[len(values) // 2 * 2 :]
    return values[0]


def place_copies(spots_ref, tables, sems):
    size = tables[0].shape[0]
    return [pltpu.make_async_copy(spots_ref.at[pl.ds(k * size, size)], table, sems.at[k]) for k, table in enumerate(tables)]


def add_rows(tables, scaled, sums, devices, first, count):
    turns = devices // GROUP
    for part in range(tables[0].shape[0] // turns):
        low, high = max(first, part * LANES), min(first + count, (part + 1) * LANES)

        def rank(r, carry):
            for turn in range(turns):
                spots = [table[part * turns + turn, 0, r] for table in tables]
                for half in range(0, GROUP, len(sums)):
                    some = range(half, half + len(sums))
                    held = [acc[pl.ds(spots[k], 1), :] for acc, k in zip(sums, some)]
                    base = part * LANES - first
                    fresh = [scaled[pl.ds(r + (base + (turn * GROUP + k) * count), 1), :] for k in some]
                    for acc, k, one, two in zip(sums, some, held, fresh):
                        acc[pl.ds(spots[k], 1), :] = one + two
            return carry

        if high > low:
            lax.fori_loop(low - part * LANES, high - part * LANES, rank, 0)


def first_kernel(slots, values_ref, spots_out, factor_ref, weight_ref, total_ref, fields, scaled, sems, *rest):
    tables, sums = rest[:GROUP], rest[GROUP:]
    devices, extended, _ = values_ref.shape
    count = extended - META
    parts = spots_out.shape[0] // devices
    fields[...] = values_ref[:, count:, :].astype(f32).reshape(devices * META, LANES)

    def field(k, start=0, step=1):
        return fields[pl.ds(start * META + k, devices // step, stride=step * META), :]

    turns = devices // GROUP
    for g in range(GROUP):
        for k in range(parts):
            high = field(k, g, GROUP)
            spot = jnp.where(high > 0.5, (high - 1.0) * 64.0 + field(parts + k, g, GROUP), float(slots)).astype(i32)
            for t in range(turns):
                spots_out[(g * parts + k) * turns + t] = spot[t : t + 1, :]
    copies = place_copies(spots_out, tables, sems)
    for copy in copies:
        copy.start()
    factor_ref[...] = field(4) + field(5) + field(6)

    clear_all(sums, slots)
    high_id = iota((slots // LANES, LANES), 0)
    low_id = iota((LANES, LANES), 0)

    def weigh(src, weight):
        factor = factor_ref[pl.ds(src, 1), :]
        scaled[pl.ds(pl.multiple_of(src * count, 8), count), :] = values_ref[src, :count, :].astype(f32) * factor
        for k in range(parts):
            spot = spots_out[(src % GROUP * parts + k) * turns + src // GROUP]
            high = ((spot >> 7) == high_id).astype(bf16)
            low = ((spot & (LANES - 1)) == low_id).astype(bf16)
            weight = weight + factor * dot_last(high, low)
        return weight

    weight_ref[...] = lax.fori_loop(0, devices, weigh, jnp.zeros((slots // LANES, LANES), f32))
    for copy in copies:
        copy.wait()
    add_rows(tables, scaled, sums, devices, 0, count)

    def merge(step, carry):
        block = pl.ds(pl.multiple_of(step * 64, 64), 64)
        total_ref[block, :] = merged([acc[block, :] for acc in sums])
        return carry

    lax.fori_loop(0, slots // 64, merge, 0)


def last_kernel(first, values_ref, spots_in, factor_ref, weight_ref, total_ref, image_ref, scaled, sems, *rest):
    tables, sums = rest[:GROUP], rest[GROUP:]
    devices, count, _ = values_ref.shape
    slots = weight_ref.shape[0] * LANES
    copies = place_copies(spots_in, tables, sems)
    copies.append(pltpu.make_async_copy(total_ref, sums[0].at[pl.ds(0, slots)], sems.at[GROUP]))
    for copy in copies:
        copy.start()
    clear_all(sums[1:], slots)

    def weigh(src, carry):
        factor = factor_ref[pl.ds(src, 1), :]
        scaled[pl.ds(pl.multiple_of(src * count, 8), count), :] = values_ref[src].astype(f32) * factor
        return carry

    lax.fori_loop(0, devices, weigh, 0)
    for copy in copies:
        copy.wait()
    add_rows(tables, scaled, sums, devices, first, count)
    for h in range(weight_ref.shape[0]):
        block = slice(h * LANES, (h + 1) * LANES)
        scale = jnp.broadcast_to(jnp.maximum(weight_ref[h : h + 1, :], 1.0), (LANES, LANES)).T
        image_ref[block, :] = merged([acc[block, :] for acc in sums]) / scale


def body(raw_pixels, kernel_bank, kernel_ids, inv_var, gap_start, warp_tile, warp_offset):
    _, rows, cols = raw_pixels.shape
    segs = cols // LANES
    axes = ("expo", "fp")
    devices = lax.axis_size("expo") * lax.axis_size("fp")
    pieces = rows * segs
    capacity = 2 * pieces // devices
    capacity1 = capacity // 4
    capacity0 = capacity - capacity1
    parts = -(-capacity // LANES)
    slots = pieces
    shape = jax.ShapeDtypeStruct

    raw = raw_pixels[0]
    above, below = halo(raw, "fp")
    tiles = jnp.transpose(warp_tile[0], (1, 2, 0))
    offsets = jnp.transpose(warp_offset[0], (1, 0))
    tall = -(-(rows + 2 * EDGE) // LANES) * LANES
    dest, meta, tv, th = pl.pallas_call(
        functools.partial(route_kernel, capacity),
        out_shape=(
            pltpu.VMEM((pieces // LANES, 1, LANES), i32),
            pltpu.VMEM((devices * META, LANES), bf16),
            pltpu.VMEM((rows, tall), bf16),
            pltpu.VMEM((2 * LANES, 4 * LANES), bf16),
        ),
        in_specs=[VMEM] * 6,
        out_specs=(VMEM,) * 4,
        scratch_shapes=[pltpu.VMEM((2, 4 * LANES), f32)],
        cost_estimate=cost(400_000_000, 600_000),
        compiler_params=params(16),
        name="route",
    )(far(tiles), far(offsets), gap_start, inv_var, kernel_ids, far(kernel_bank))

    send0, send1 = pl.pallas_call(
        pack_kernel,
        out_shape=(
            pltpu.VMEM((devices, capacity0 + META, LANES), bf16),
            pltpu.VMEM((devices, capacity1, LANES), bf16),
        ),
        in_specs=[ANY, ANY, ANY, VMEM, VMEM, VMEM, VMEM],
        out_specs=(VMEM, VMEM),
        scratch_shapes=[
            pltpu.VMEM((rows + 2 * EDGE, cols), bf16),
            pltpu.VMEM((rows, cols + 2 * LANES), bf16),
            pltpu.VMEM((pieces, LANES), f32),
            pltpu.VMEM((devices * capacity + 8, LANES), f32),
            pltpu.SemaphoreType.DMA((3 + pieces // LANES,)),
        ]
        + [pltpu.SMEM((1, 1, LANES), i32)] * (pieces // LANES),
        cost_estimate=cost(10_000_000_000, 4_000_000),
        compiler_params=params(24),
        name="pack",
    )(far(raw), near(above), near(below), near(tv), near(th), near(dest), near(meta))

    got0 = lax.all_to_all(send0, axes, split_axis=0, concat_axis=0, tiled=True)
    got1 = lax.all_to_all(send1, axes, split_axis=0, concat_axis=0, tiled=True)

    tables = [pltpu.SemaphoreType.DMA((GROUP + 1,))] + [pltpu.SMEM((parts * devices // GROUP, 1, LANES), i32)] * GROUP
    spots, factor, weight, total = pl.pallas_call(
        functools.partial(first_kernel, slots),
        out_shape=(
            pltpu.VMEM((parts * devices, 1, LANES), i32),
            pltpu.VMEM((devices, LANES), f32),
            pltpu.VMEM((slots // LANES, LANES), f32),
            pltpu.HBM((slots, LANES), f32),
        ),
        in_specs=[VMEM],
        out_specs=(VMEM,) * 4,
        scratch_shapes=[
            pltpu.VMEM((devices * META, LANES), f32),
            pltpu.VMEM((devices * capacity0, LANES), f32),
            *tables,
        ]
        + [pltpu.VMEM((slots + 8, LANES), f32)] * SPLIT[0],
        cost_estimate=cost(10_000_000_000, 4_000_000),
        compiler_params=params(28),
        name="sum_first",
    )(near(got0))
    image = pl.pallas_call(
        functools.partial(last_kernel, capacity0),
        out_shape=shape((slots, LANES), f32),
        in_specs=[VMEM] * 4 + [ANY],
        out_specs=VMEM,
        scratch_shapes=[pltpu.VMEM((devices * capacity1, LANES), f32), *tables]
        + [pltpu.VMEM((slots + 8, LANES), f32)] * SPLIT[1],
        cost_estimate=cost(10_000_000_000, 4_000_000),
        compiler_params=params(20),
        name="sum_last",
    )(near(got1), near(spots), near(factor), near(weight), far(total))
    return image[None], weight.reshape(1, slots)


def solution(mesh):
    in_specs = (
        P("expo", "fp", None),
        P(),
        P("expo", "fp"),
        P("expo", "fp"),
        P("expo", "fp"),
        P("expo", "fp", None, None),
        P("expo", "fp", None),
    )
    out_specs = (P(("expo", "fp"), None, None), P(("expo", "fp"), None))
    return jax.shard_map(body, mesh=mesh, in_specs=in_specs, out_specs=out_specs, check_vma=False)
```

time: 112 us -> 91.8 us (0.82)
  waiting for transfers between devices: 48.8 us -> 0.01 us
  blocking collectives: 0 us -> 47.2 us
  starting transfers between devices: 17.5 us -> 6.94 us
  local copies, waits for them, and re-layouts: 7.03 us -> 1.6 us
  other arithmetic: 1.37 us -> 0 us
    all_to_all x2 -> x1, waiting for transfers between devices: 48.7 us -> 0.01 us  [body(): got1 = lax.all_to_all(send1, axes, split_axis=0, concat_axis=0, tiled=True)]
    all_to_all x0 -> x1, blocking collectives: none -> 47.2 us  [body(): got0 = lax.all_to_all(send0, axes, split_axis=0, concat_axis=0, tiled=True)]
    all_to_all x2 -> x1, starting transfers between devices: 13.2 us -> 2.61 us  [body(): got1 = lax.all_to_all(send1, axes, split_axis=0, concat_axis=0, tiled=True)]
    unnamed x11 -> x1, local copies, waits for them, and re-layouts: 3.99 us -> 0.61 us
    all_to_all x1 -> x0, local copies, waits for them, and re-layouts: 1.44 us -> none  [body(): lax.all_to_all(meta, axes, split_axis=0, concat_axis=0, tiled=True)]
    pad x1 -> x0, other arithmetic: 1.36 us -> none  [body(): jnp.pad(kernel_bank.astype(f32), ((0, 0), (0, 0), (lead, LANES - taps - l...]
    pallas_call x3 -> x4, Pallas kernels: 33.3 us -> 33 us  [the longest x1 16.1 us: body(): pl.pallas_call(functools.partial(first_kernel, slots), out_shape=(pltpu.V...]
  transfers between devices with their start and end apart: 4 -> 3, of which waited for: 1 -> 0; matrix products, arithmetic and copies ran while one was open for 4% -> 1% of each run, Pallas kernels for 11% -> 21%
where the time goes in v2:
time: 91.8 us; the launch traced here: 91.4 us
  blocking collectives  47.2 us (51%)
  Pallas kernels  33 us (36%)
  starting transfers between devices  6.94 us (8%)
  between operations  2.64 us (3%)
  local copies, waits for them, and re-layouts  1.6 us (2%)
    all_to_all x1, blocking collectives, body(): got0 = lax.all_to_all(send0, axes, split_axis=0, concat_axis=0, tiled=True)  47.2 us
    pallas_call x1, Pallas kernels, body(): pl.pallas_call(functools.partial(first_kernel, slots), out_shape=(pltpu.V...  16.1 us
    pallas_call x1, Pallas kernels, body(): pl.pallas_call(functools.partial(last_kernel, capacity0), out_shape=shape...  7.19 us
    pallas_call x1, Pallas kernels, body(): pl.pallas_call(pack_kernel, out_shape=(pltpu.VMEM((devices, capacity0 + M...  6.9 us
    ppermute x1, starting transfers between devices, halo(): above = lax.ppermute(shard[-EDGE:], axis, up)  3.04 us
    pallas_call x1, Pallas kernels, body(): pl.pallas_call(functools.partial(route_kernel, capacity), out_shape=(pltp...  2.76 us
    all_to_all x1, starting transfers between devices, body(): got1 = lax.all_to_all(send1, axes, split_axis=0, concat_axis=0, tiled=True)  2.61 us
  transfers between devices with their start and end apart: 3, of which 0 were waited for; matrix products, arithmetic and copies ran while one was open for 1% of the time, Pallas kernels for 21%

profile of v2, /device:TPU:0, one launch (start us, length us, event | category | flops | bytes accessed | tf_op | source)
XLA Modules:
  0.0 91.4 jit_solution(9166928802650045181)
XLA Ops:
  0.6 1.0 %slice_bitcast_fusion = (bf16[32,2048]{1,0:T(8,128)(2,1)S(1)}, bf16[32,2048]{1,0:T(8,128)(2,1)S(1)}) fusion(bf16[1,256,2048]{2,1,0:T(8,128)(2,1)} %param.7), kind=kLoop, calls=%fused_computation | loop fusion | bytes 524288 | tf_op jit(solution)/shard_map/slice | solution.py:51
  1.6 1.3 %collective-permute-start.1 = (bf16[32,2048]{1,0:T(8,128)(2,1)S(1)}, bf16[32,2048]{1,0:T(8,128)(2,1)S(1)}, u32[]{:S(2)}, u32[]{:S(2)}) collective-permute-start(bf16[32,2048]{1,0:T(8,128)(2,1)S(1)} %get-tuple-element.22), channel_id=1, source_target_pairs={{1,0},{2,1},{3,2},{4,3},{5,4},{6,5},{7,6},{9,8},{10,9},{11,10},{12... | collective-permute-start | bytes 393224 | tf_op jit(solution)/shard_map/ppermute | solution.py:51
  2.9 3.0 %collective-permute-start = (bf16[32,2048]{1,0:T(8,128)(2,1)S(1)}, bf16[32,2048]{1,0:T(8,128)(2,1)S(1)}, u32[]{:S(2)}, u32[]{:S(2)}) collective-permute-start(bf16[32,2048]{1,0:T(8,128)(2,1)S(1)} %get-tuple-element.23), channel_id=1, source_target_pairs={{0,1},{1,2},{2,3},{3,4},{4,5},{5,6},{6,7},{8,9},{9,10},{10,11},{11... | collective-permute-start | bytes 393224 | tf_op jit(solution)/shard_map/ppermute | solution.py:50
  7.9 2.8 %route.1 = (s32[32,1,128]{2,1,0:T(1,128)S(1)}, bf16[256,128]{1,0:T(8,128)(2,1)S(1)}, bf16[256,384]{1,0:T(8,128)(2,1)S(1)}, bf16[256,512]{1,0:T(8,128)(2,1)S(1)}) custom-call(s32[16,1,256]{2,1,0:T(1,128)} %bitcast.15, s32[16,256]{1,0:T(8,128)} %bitcast.16, s32[1,1]{1,0:T(1,128)S(6)} %copy.12.gap_ref, f32[1,1]{1,0:T(1,128)S(6)} %copy.11.var_ref, ...), custom_call_target="tpu_custom_call" | custom-call | flops 400000000 | bytes 600000 | tf_op jit(solution)/shard_map/route/pallas_call | solution.py:291
  10.7 0.0 collective-permute-done.1.below_ref
  10.7 0.0 collective-permute-done.above_ref
  10.7 6.9 %pack.1 = (bf16[32,200,128]{2,1,0:T(8,128)(2,1)S(1)}, bf16[32,64,128]{2,1,0:T(8,128)(2,1)}) custom-call(bf16[256,2048]{1,0:T(8,128)(2,1)} %bitcast.14, bf16[32,2048]{1,0:T(8,128)(2,1)S(1)} %collective-permute-done.above_ref, bf16[32,2048]{1,0:T(8,128)(2,1)S(1)} %collective-permute-done.1.below_ref, bf16[256,384]{1,0:T(8,128)(2,1)S(1)} %get-tuple-element.12.tv_ref, ...), custom_call_target="tpu_custom_call" | custom-call | flops 10000000000 | bytes 4000000 | tf_op jit(solution)/shard_map/pack/pallas_call | solution.py:307
  17.6 47.2 %all_to_all.10.values_ref = bf16[32,200,128]{2,1,0:T(8,128)(2,1)S(1)} all-to-all(bf16[32,200,128]{2,1,0:T(8,128)(2,1)S(1)} %get-tuple-element.17), channel_id=1, replica_groups=mesh['expo'=4,'fp'=8] {'expo','fp'}, dimensions={0} | all-to-all | bytes 3276800 | tf_op jit(solution)/shard_map/all_to_all | solution.py:328
  64.8 2.6 %all-to-all-start = ((bf16[32,64,128]{2,1,0:T(8,128)(2,1)}), bf16[32,64,128]{2,1,0:T(8,128)(2,1)S(1)}, u32[]{:S(2)}, u32[]{:S(2)}) async-start(bf16[32,64,128]{2,1,0:T(8,128)(2,1)} %get-tuple-element.16), calls=%async_computation | async-start | bytes 1048576 | tf_op jit(solution)/shard_map/all_to_all | solution.py:329
  67.5 16.1 %sum_first.1 = (s32[64,1,128]{2,1,0:T(1,128)S(1)}, f32[32,128]{1,0:T(8,128)S(1)}, f32[32,128]{1,0:T(8,128)S(1)}, f32[4096,128]{1,0:T(8,128)}) custom-call(bf16[32,200,128]{2,1,0:T(8,128)(2,1)S(1)} %all_to_all.10.values_ref), custom_call_target="tpu_custom_call" | custom-call | flops 10000000000 | bytes 4000000 | tf_op jit(solution)/shard_map/sum_first/pallas_call | solution.py:332
  83.6 0.6 copy.9
  84.2 0.0 all-to-all-done.values_ref
  84.2 7.2 %sum_last.1 = f32[4096,128]{1,0:T(8,128)} custom-call(bf16[32,64,128]{2,1,0:T(8,128)(2,1)S(1)} %all-to-all-done.values_ref, s32[64,1,128]{2,1,0:T(1,128)S(1)} %get-tuple-element.18.spots_in, f32[32,128]{1,0:T(8,128)S(1)} %get-tuple-element.19.factor_ref, f32[32,128]{1,0:T(8,128)S(1)} %get-tuple-element.20.weight_ref, f32[4096,128]{1,0:T(8,128)} %get-tuple-element.21.total_ref), custom_call_target="tpu_custom_call" | custom-call | flops 10000000000 | bytes 4000000 | tf_op jit(solution)/shard_map/sum_last/pallas_call | solution.py:352
Async XLA Ops:
  1.6 9.1 %collective-permute-start.1 = (bf16[32,2048]{1,0:T(8,128)(2,1)S(1)}, bf16[32,2048]{1,0:T(8,128)(2,1)S(1)}, u32[]{:S(2)}, u32[]{:S(2)}) collective-permute-start(bf16[32,2048]{1,0:T(8,128)(2,1)S(1)} %get-tuple-element.22), channel_id=1, source_target_pairs={{1,0},{2,1},{3,2},{4,3},{5,4},{6,5},{7,6},{9,8},{10,9},{11,10},{12... | collective-permute-start | bytes 393224 | tf_op jit(solution)/shard_map/ppermute | solution.py:51
  2.9 7.8 %collective-permute-start = (bf16[32,2048]{1,0:T(8,128)(2,1)S(1)}, bf16[32,2048]{1,0:T(8,128)(2,1)S(1)}, u32[]{:S(2)}, u32[]{:S(2)}) collective-permute-start(bf16[32,2048]{1,0:T(8,128)(2,1)S(1)} %get-tuple-element.23), channel_id=1, source_target_pairs={{0,1},{1,2},{2,3},{3,4},{4,5},{5,6},{6,7},{8,9},{9,10},{10,11},{11... | collective-permute-start | bytes 393224 | tf_op jit(solution)/shard_map/ppermute | solution.py:50
  64.8 19.4 %all-to-all-start = ((bf16[32,64,128]{2,1,0:T(8,128)(2,1)}), bf16[32,64,128]{2,1,0:T(8,128)(2,1)S(1)}, u32[]{:S(2)}, u32[]{:S(2)}) async-start(bf16[32,64,128]{2,1,0:T(8,128)(2,1)} %get-tuple-element.16), calls=%async_computation | async-start | bytes 1048576 | tf_op jit(solution)/shard_map/all_to_all | solution.py:329
